TPU v7x, 256 devices: a whole 4x4x8 slice. The times are simulated.
256 devices in a mesh: row: 16 (over y_lo, x, core), col: 16 (over z, y_hi).
Axes of the slice: x: 4, y: 4 (y_hi: 2, y_lo: 2; y = y_hi * 2 + y_lo), z: 8, core: 2. Of those that a mesh axis runs over, the one named last changes fastest.
Arguments:
- row_frames: float32 [3, 8192, 256], P(None, ('row', 'col')), may hold values from -40 to 40, as said below
- col_frames: float32 [3, 8192, 256], P(None, ('col', 'row')), may hold values from -40 to 40, as said below
- vectors: float32 [64, 8192], P(None, ('col', 'row')), may hold values from -6 to 6
Outputs:
- embedding_product: float32 [64, 8192], P(None, ('row', 'col'))
Inputs may be any that keep to these rules, and one draw needn't show every extreme that they name: `row_frames`: frames of one chain of 256 atoms, each rigidly rotated and moved and perturbed by its own amount. `col_frames`: frames of one chain of 256 atoms, each rigidly rotated and moved and perturbed by its own amount.
All inputs are finite; a program needn't handle non-finite values.
Results may differ from a plain program's by a relative error of at most 0.00017.
Values sent between devices are 32-bit elements; how exact they have to be, the bound alone decides.
A program may use at most 64 MiB of HBM per device.

v0:
```python
import jax
import jax.numpy as jnp
from jax import lax
from jax.sharding import PartitionSpec as P

NEWTON = 8
band_width = 2.0


def centre(frames):
    return frames - jnp.mean(frames, axis=2, keepdims=True)


def kernel_tile(rows, cols):
    count_rows = rows.shape[1]
    count_cols = cols.shape[1]
    atoms = rows.shape[2]
    row_norms = jnp.sum(rows * rows, axis=(0, 2))
    col_norms = jnp.sum(cols * cols, axis=(0, 2))
    product = jnp.dot(
        cols.reshape(3 * count_cols, atoms),
        rows.reshape(3 * count_rows, atoms).T,
        precision=lax.Precision.HIGHEST,
        preferred_element_type=jnp.float32,
    )
    product = product.reshape(3, count_cols, 3, count_rows)
    moment = [[product[second, :, first, :] for second in range(3)] for first in range(3)]
    half_norm = 0.5 * (row_norms[None, :] + col_norms[:, None])
    coef_two = -2.0 * sum(
        (moment[first][second] * moment[first][second] for first in range(3) for second in range(3))
    )
    coef_one = 8.0 * (
        moment[0][0] * moment[1][2] * moment[2][1]
        + moment[1][1] * moment[2][0] * moment[0][2]
        + moment[2][2] * moment[0][1] * moment[1][0]
    ) - 8.0 * (
        moment[0][0] * moment[1][1] * moment[2][2]
        + moment[1][2] * moment[2][0] * moment[0][1]
        + moment[2][1] * moment[1][0] * moment[0][2]
    )
    trace_one = moment[0][0] + moment[1][1] + moment[2][2]
    key_matrix = [
        [
            trace_one,
            moment[1][2] - moment[2][1],
            moment[2][0] - moment[0][2],
            moment[0][1] - moment[1][0],
        ],
        [
            moment[1][2] - moment[2][1],
            moment[0][0] - moment[1][1] - moment[2][2],
            moment[0][1] + moment[1][0],
            moment[2][0] + moment[0][2],
        ],
        [
            moment[2][0] - moment[0][2],
            moment[0][1] + moment[1][0],
            -moment[0][0] + moment[1][1] - moment[2][2],
            moment[1][2] + moment[2][1],
        ],
        [
            moment[0][1] - moment[1][0],
            moment[2][0] + moment[0][2],
            moment[1][2] + moment[2][1],
            -moment[0][0] - moment[1][1] + moment[2][2],
        ],
    ]
    minor_top = [
        key_matrix[0][0] * key_matrix[1][1] - key_matrix[1][0] * key_matrix[0][1],
        key_matrix[0][0] * key_matrix[1][2] - key_matrix[1][0] * key_matrix[0][2],
        key_matrix[0][0] * key_matrix[1][3] - key_matrix[1][0] * key_matrix[0][3],
        key_matrix[0][1] * key_matrix[1][2] - key_matrix[1][1] * key_matrix[0][2],
        key_matrix[0][1] * key_matrix[1][3] - key_matrix[1][1] * key_matrix[0][3],
        key_matrix[0][2] * key_matrix[1][3] - key_matrix[1][2] * key_matrix[0][3],
    ]
    minor_low = [
        key_matrix[2][0] * key_matrix[3][1] - key_matrix[3][0] * key_matrix[2][1],
        key_matrix[2][0] * key_matrix[3][2] - key_matrix[3][0] * key_matrix[2][2],
        key_matrix[2][0] * key_matrix[3][3] - key_matrix[3][0] * key_matrix[2][3],
        key_matrix[2][1] * key_matrix[3][2] - key_matrix[3][1] * key_matrix[2][2],
        key_matrix[2][1] * key_matrix[3][3] - key_matrix[3][1] * key_matrix[2][3],
        key_matrix[2][2] * key_matrix[3][3] - key_matrix[3][2] * key_matrix[2][3],
    ]
    coef_zero = (
        minor_top[0] * minor_low[5]
        - minor_top[1] * minor_low[4]
        + minor_top[2] * minor_low[3]
        + minor_top[3] * minor_low[2]
        - minor_top[4] * minor_low[1]
        + minor_top[5] * minor_low[0]
    )
    eigen = half_norm
    for newton_step in range(NEWTON):
        eigen_sq = eigen * eigen
        value = (eigen_sq + coef_two) * eigen_sq + coef_one * eigen + coef_zero
        slope = 4.0 * eigen_sq * eigen + 2.0 * coef_two * eigen + coef_one
        eigen = eigen - value / slope
    squared = jnp.maximum(2.0 * (half_norm - eigen) / atoms, 0.0)
    return jnp.exp(-squared / band_width)


def per_device(row_frames, col_frames, vectors):
    rows_own = centre(row_frames)
    cols_own = centre(col_frames)
    panel_rows = lax.all_gather(rows_own, "col", axis=1, tiled=True)
    tile = kernel_tile(panel_rows, lax.all_gather(cols_own, "row", axis=1, tiled=True))
    weighted = jnp.dot(
        lax.all_gather(vectors, "row", axis=1, tiled=True),
        tile,
        precision=lax.Precision.HIGHEST,
        preferred_element_type=jnp.float32,
    )
    degree = jnp.sum(tile, axis=0, keepdims=True)
    summed, total = (
        lax.psum_scatter(weighted, "col", scatter_dimension=1, tiled=True),
        lax.psum_scatter(degree, "col", scatter_dimension=1, tiled=True),
    )
    return summed / total


def solution(mesh):
    return jax.shard_map(
        per_device,
        mesh=mesh,
        in_specs=(
            P(None, ("row", "col"), None),
            P(None, ("col", "row"), None),
            P(None, ("col", "row")),
        ),
        out_specs=P(None, ("row", "col")),
        check_vma=False,
    )
```

profile of v0, /device:TPU:2, one launch (start us, length us, event | category | flops | bytes accessed | tf_op | source)
XLA Modules:
  0.0 559.0 jit_solution(16649390457122390750)
XLA Ops:
  6.5 0.0 all-gather.5.cloned.1.call-start
  6.5 1.0 reduce_sum.47
  7.5 1.6 broadcast_subtract_fusion
  9.1 0.0 all-gather.5.cloned.1.call-update
  9.2 0.0 all-gather.3.cloned.1.call-start
  9.2 1.0 reduce_sum.45
  10.2 1.6 broadcast_subtract_fusion.1
  11.8 0.0 all-gather.3.cloned.1.call-update
  11.8 0.0 reduce-scatter.9.cloned.1.call-start
  11.9 19.1 %all_gather.11 = f32[64,512]{0,1:T(8,128)S(1)} all-gather(f32[64,32]{0,1:T(8,128)} %param.5), channel_id=1, replica_groups=mesh['row'=16,'col'=16] {'row'}, dimensions={1}, use_global_device_ids=true | all-gather | bytes 139264 | tf_op jit(solution)/shard_map/all_gather | solution.py:108
  31.0 16.7 %all-gather.5.cloned.1.call-done = f32[3,512,256]{2,1,0:T(8,128)} async-done(((f32[3,32,256]{2,1,0:T(8,128)}), f32[3,512,256]{2,1,0:T(8,128)}) %all-gather.5.cloned.1.call-update) | async-done | bytes 1572880 | tf_op jit(solution)/shard_map/all_gather | solution.py:106
  47.7 0.0 copy-start
  47.7 1.7 multiply_reduce_fusion
  49.4 83.5 %all-gather.3.cloned.1.call-done = f32[3,512,256]{2,1,0:T(8,128)} async-done(((f32[3,32,256]{2,1,0:T(8,128)}), f32[3,512,256]{2,1,0:T(8,128)}) %all-gather.3.cloned.1.call-update) | async-done | bytes 1572880 | tf_op jit(solution)/shard_map/all_gather | solution.py:105
  132.9 0.0 copy-done
  132.9 0.0 copy-start.1
  132.9 9.8 %fusion = f32[3,512,3,512]{3,1,2,0:T(8,128)S(1)} fusion(f32[3,512,256]{2,1,0:T(8,128)S(1)} %copy-done, f32[3,512,256]{2,1,0:T(8,128)} %all-gather.3.cloned.1.call-done), kind=kOutput, calls=%fused_computation | convolution fusion | flops 7247757312 | bytes 12582912 | tf_op jit(solution)/shard_map/dot_general | solution.py:20
  142.7 0.0 copy-done.1
  142.7 0.2 multiply_reduce_fusion.1
  142.9 8.1 %fusion.42 = (f32[512]{0:T(512)S(1)}, f32[512,512]{1,0:T(8,128)S(1)}) fusion(f32[3,512,3,512]{3,1,2,0:T(8,128)S(1)} %fusion, f32[512]{0:T(512)S(1)} %multiply_reduce_fusion, f32[512]{0:T(512)S(1)} %multiply_reduce_fusion.1), kind=kLoop, calls=%fused_computation.77 | loop fusion | flops 52690432 | bytes 10491904 | tf_op jit(solution)/shard_map/reduce_sum | solution.py:113
  151.0 0.9 copy.10
  151.9 0.0 reduce-scatter.9.cloned.1.call-update
  151.9 0.0 reduce-scatter.7.cloned.1.call-start
  151.9 0.8 convolution_bitcast_fusion
  152.7 0.8 copy.8
  153.6 0.0 reduce-scatter.7.cloned.1.call-update
  153.6 195.3 %reduce-scatter.9.cloned.1.call-done = f32[32,1]{1,0:T(8,128)} async-done(((f32[512,1]{1,0:T(8,128)}), f32[32,1]{1,0:T(8,128)}) %reduce-scatter.9.cloned.1.call-update) | async-done | bytes 144
  348.9 0.8 copy.11
  349.7 201.4 %reduce-scatter.7.cloned.1.call-done = f32[32,64]{1,0:T(8,128)} async-done(((f32[512,64]{1,0:T(8,128)}), f32[32,64]{1,0:T(8,128)}) %reduce-scatter.7.cloned.1.call-update) | async-done | bytes 8208
  551.0 1.4 bitcast_divide_fusion
  (2 shorter events, 0.0 us)
Async XLA Ops:
  6.5 41.1 %all-gather.5.cloned.1.call-start = ((), (), s32[]{:S(2)}) async-start(), calls=%async_computation.3 | async-start | bytes 1671168 | tf_op jit(solution)/shard_map/all_gather | solution.py:106
  9.2 123.7 %all-gather.3.cloned.1.call-start = ((), (), s32[]{:S(2)}) async-start(), calls=%async_computation.2 | async-start | bytes 1671168 | tf_op jit(solution)/shard_map/all_gather | solution.py:105
  11.8 337.0 %reduce-scatter.9.cloned.1.call-start = ((), (), s32[]{:S(2)}) async-start(), calls=%async_computation.5 | async-start | bytes 278528
  47.7 85.2 %copy-start = (f32[3,512,256]{2,1,0:T(8,128)S(1)}, f32[3,512,256]{2,1,0:T(8,128)}, u32[]{:S(2)}) copy-start(f32[3,512,256]{2,1,0:T(8,128)} %all-gather.5.cloned.1.call-done) | copy-start | bytes 4718596
  132.9 9.8 %copy-start.1 = (f32[3,512,256]{2,1,0:T(8,128)S(1)}, f32[3,512,256]{2,1,0:T(8,128)}, u32[]{:S(2)}) copy-start(f32[3,512,256]{2,1,0:T(8,128)} %all-gather.3.cloned.1.call-done) | copy-start | bytes 4718596
  151.9 399.1 %reduce-scatter.7.cloned.1.call-start = ((), (), s32[]{:S(2)}) async-start(), calls=%async_computation.4 | async-start | bytes 278528
Sparse Core Ops, SparseCore 0:
  9.3 38.3 all-gather.4
  50.3 82.5 all-gather.2
  152.0 196.8 reduce-scatter.8
  353.0 198.0 reduce-scatter.6
where the time goes:
time: 559 us
  waiting for transfers between devices  497 us (89%)
  blocking collectives  19.1 us (3%)
  other arithmetic  16.6 us (3%)
  between operations  13.2 us (2%)
  matrix products  10.6 us (2%)
    unnamed x6, waiting for transfers between devices  397 us
    all_gather x1, waiting for transfers between devices, per_device(): panel_rows = lax.all_gather(rows_own, 'col', axis=1, tiled=True)  83.5 us
    all_gather x1, blocking collectives, per_device(): lax.all_gather(vectors, 'row', axis=1, tiled=True)  19.1 us
    all_gather x1, waiting for transfers between devices, per_device(): lax.all_gather(cols_own, 'row', axis=1, tiled=True)  16.7 us
  transfers between devices with their start and end apart: 4, of which 4 were waited for; matrix products, arithmetic and copies ran while one was open for 1% of the time, Pallas kernels for 0%

commit v1 on v0

--- a/solution.py
+++ b/solution.py
@@ -2,6 +2,7 @@
 import jax.numpy as jnp
 from jax import lax
 from jax.sharding import PartitionSpec as P
+from jax.lax import all_to_all, axis_size
 
 NEWTON = 8
 band_width = 2.0
@@ -100,10 +101,16 @@
 
 
 def per_device(row_frames, col_frames, vectors):
+
+    def group_mark(field_in):
+        return jnp.concatenate(
+            all_to_all(jnp.stack([field_in for _ in range(axis_size("row"))], 0), "row", 0, 0), 1
+        )
+
     rows_own = centre(row_frames)
     cols_own = centre(col_frames)
     panel_rows = lax.all_gather(rows_own, "col", axis=1, tiled=True)
-    tile = kernel_tile(panel_rows, lax.all_gather(cols_own, "row", axis=1, tiled=True))
+    tile = kernel_tile(panel_rows, group_mark(cols_own))
     weighted = jnp.dot(
         lax.all_gather(vectors, "row", axis=1, tiled=True),
         tile,

time: 559 us -> 527 us (0.943)
  waiting for transfers between devices: 497 us -> 445 us
  blocking collectives: 19.1 us -> 32.6 us
  starting transfers between devices: 0.13 us -> 6.07 us
    all_gather x1, waiting for transfers between devices: 83.5 us -> 48.9 us  [per_device(): panel_rows = lax.all_gather(rows_own, 'col', axis=1, tiled=True)]
    all_gather x1 -> x0, waiting for transfers between devices: 16.7 us -> none  [per_device(): lax.all_gather(cols_own, 'row', axis=1, tiled=True)]
    all_gather x1, blocking collectives: 19.1 us -> 32.6 us  [per_device(): lax.all_gather(vectors, 'row', axis=1, tiled=True)]
    all_to_all x0 -> x1, starting transfers between devices: none -> 5.99 us  [group_mark(): all_to_all(jnp.stack([field_in for _ in range(axis_size('row'))], 0), 'ro...]
    unnamed x6 -> x5, waiting for transfers between devices: 397 us -> 397 us
  transfers between devices with their start and end apart: 4 -> 4, of which waited for: 4 -> 3; matrix products, arithmetic and copies ran while one was open for 1% -> 1% of each run, Pallas kernels for 0% -> 0%
where the time goes in v1:
time: 527 us
  waiting for transfers between devices  445 us (84%)
  blocking collectives  32.6 us (6%)
  other arithmetic  16 us (3%)
  between operations  13.2 us (3%)
  matrix products  9.04 us (2%)
  starting transfers between devices  6.07 us (1%)
    unnamed x5, waiting for transfers between devices  397 us
    all_gather x1, waiting for transfers between devices, per_device(): panel_rows = lax.all_gather(rows_own, 'col', axis=1, tiled=True)  48.9 us
    all_gather x1, blocking collectives, per_device(): lax.all_gather(vectors, 'row', axis=1, tiled=True)  32.6 us
  transfers between devices with their start and end apart: 4, of which 3 were waited for; matrix products, arithmetic and copies ran while one was open for 1% of the time, Pallas kernels for 0%

profile of v1, /device:TPU:2, one launch (start us, length us, event | category | flops | bytes accessed | tf_op | source)
XLA Modules:
  0.0 526.6 jit_solution(10172562669899155118)
XLA Ops:
  6.5 0.0 all-gather.2.cloned.1.call-start
  6.5 1.0 reduce_sum.45
  7.5 1.6 broadcast_subtract_fusion.1
  9.1 0.0 all-gather.2.cloned.1.call-update
  9.2 1.0 reduce_sum.47
  10.2 1.0 broadcast_subtract_fusion
  11.1 1.3 stack.2
  12.5 0.0 copy-start.1
  12.5 6.0 %all-to-all-start = ((f32[16,3,32,256]{3,2,1,0:T(8,128)}), f32[16,3,32,256]{3,2,1,0:T(8,128)S(1)}, u32[]{:S(2)}, u32[]{:S(2)}) async-start(f32[16,3,32,256]{3,2,1,0:T(8,128)} %stack.2), calls=%async_computation | async-start | bytes 3145728 | tf_op jit(solution)/shard_map/all_to_all | solution.py:107
  18.5 0.0 reduce-scatter.9.cloned.1.call-start
  18.5 0.0 copy-done.1
  18.5 32.6 %all_gather.7 = f32[64,512]{0,1:T(8,128)S(1)} all-gather(f32[64,32]{0,1:T(8,128)S(1)} %copy-done.1), channel_id=1, replica_groups=mesh['row'=16,'col'=16] {'row'}, dimensions={1}, use_global_device_ids=true | all-gather | bytes 139264 | tf_op jit(solution)/shard_map/all_gather | solution.py:115
  51.1 0.0 all-to-all-done
  51.1 0.2 multiply_reduce_fusion
  51.3 0.1 add.209
  51.4 0.2 copy.7
  51.6 48.9 %all-gather.2.cloned.1.call-done = f32[3,512,256]{2,1,0:T(8,128)} async-done(((f32[3,32,256]{2,1,0:T(8,128)}), f32[3,512,256]{2,1,0:T(8,128)}) %all-gather.2.cloned.1.call-update) | async-done | bytes 1572880 | tf_op jit(solution)/shard_map/all_gather | solution.py:112
  100.5 0.0 copy-start
  100.5 1.7 multiply_reduce_fusion.1
  102.2 0.2 copy-done
  102.4 8.3 %fusion = f32[3,512,3,512]{3,1,2,0:T(8,128)S(1)} fusion(f32[3,512,256,1]{2,1,3,0:T(8,128)S(1)} %bitcast.86, f32[3,512,256]{2,1,0:T(8,128)S(1)} %copy-done), kind=kOutput, calls=%fused_computation | convolution fusion | flops 7247757312 | bytes 12582912 | tf_op jit(solution)/shard_map/dot_general | solution.py:21
  110.6 8.1 %fusion.41 = (f32[512]{0:T(512)S(1)}, f32[512,512]{1,0:T(8,128)S(1)}) fusion(f32[3,512,3,512]{3,1,2,0:T(8,128)S(1)} %fusion, f32[512]{0:T(512)S(1)} %add.209, f32[512]{0:T(512)S(1)} %multiply_reduce_fusion.1), kind=kLoop, calls=%fused_computation.76 | loop fusion | flops 52690432 | bytes 10491904 | tf_op jit(solution)/shard_map/reduce_sum | solution.py:120
  118.8 0.9 copy.12
  119.6 0.0 reduce-scatter.9.cloned.1.call-update
  119.6 0.0 reduce-scatter.7.cloned.1.call-start
  119.7 0.8 convolution_bitcast_fusion
  120.5 0.8 copy.10
  121.3 0.0 reduce-scatter.7.cloned.1.call-update
  121.3 195.1 %reduce-scatter.9.cloned.1.call-done = f32[32,1]{1,0:T(8,128)} async-done(((f32[512,1]{1,0:T(8,128)}), f32[32,1]{1,0:T(8,128)}) %reduce-scatter.9.cloned.1.call-update) | async-done | bytes 144
  316.4 0.8 copy.13
  317.2 201.4 %reduce-scatter.7.cloned.1.call-done = f32[32,64]{1,0:T(8,128)} async-done(((f32[512,64]{1,0:T(8,128)}), f32[32,64]{1,0:T(8,128)}) %reduce-scatter.7.cloned.1.call-update) | async-done | bytes 8208
  518.6 1.4 bitcast_divide_fusion
  (2 shorter events, 0.0 us)
Async XLA Ops:
  6.5 93.9 %all-gather.2.cloned.1.call-start = ((), (), s32[]{:S(2)}) async-start(), calls=%async_computation.3 | async-start | bytes 1671168 | tf_op jit(solution)/shard_map/all_gather | solution.py:112
  12.5 6.0 %copy-start.1 = (f32[64,32]{0,1:T(8,128)S(1)}, f32[64,32]{0,1:T(8,128)}, u32[]{:S(2)}) copy-start(f32[64,32]{0,1:T(8,128)} %param.5) | copy-start | bytes 24580
  12.5 38.7 %all-to-all-start = ((f32[16,3,32,256]{3,2,1,0:T(8,128)}), f32[16,3,32,256]{3,2,1,0:T(8,128)S(1)}, u32[]{:S(2)}, u32[]{:S(2)}) async-start(f32[16,3,32,256]{3,2,1,0:T(8,128)} %stack.2), calls=%async_computation | async-start | bytes 3145728 | tf_op jit(solution)/shard_map/all_to_all | solution.py:107
  18.5 298.0 %reduce-scatter.9.cloned.1.call-start = ((), (), s32[]{:S(2)}) async-start(), calls=%async_computation.5 | async-start | bytes 278528
  100.5 1.9 copy-start
  119.6 399.0 %reduce-scatter.7.cloned.1.call-start = ((), (), s32[]{:S(2)}) async-start(), calls=%async_computation.4 | async-start | bytes 278528
Sparse Core Ops, SparseCore 0:
  10.0 90.4 all-gather.1
  119.8 196.6 reduce-scatter.8
  320.7 197.8 reduce-scatter.6
